TPU v7x, 32 devices: a whole 2x2x4 slice. The times are simulated.
32 devices in a mesh: groups: 2 (over x), seq: 16 (over z, y, core).
Axes of the slice: x: 2, y: 2, z: 4, core: 2. Of those that a mesh axis runs over, the one named last changes fastest.
Arguments:
- tokens: bfloat16 [262144, 2048], P(('groups', 'seq')), parts along dimension 0, may hold values from -6 to 6
- right_blocks: bfloat16 [256, 512, 512], P('seq'), may hold values from -0.25 to 0.25
- left_blocks: bfloat16 [512, 256, 256], P('seq'), may hold values from -0.375 to 0.375
- chan_first: bfloat16 [32, 64, 64], replicated, may hold values from -0.75 to 0.75
- chan_second: bfloat16 [64, 32, 32], replicated, may hold values from -1 to 1
Outputs:
- mixed: bfloat16 [262144, 2048], P(('groups', 'seq')), parts along dimension 0
There are 2 independent parts, one for each index of `groups`. A program takes and returns all parts, laid end to end along the dimension named above; an argument that names none is the same for every part. Nothing has to cross between parts.
All inputs are finite; a program needn't handle non-finite values.
Results may differ from a plain program's by a relative error of at most 0.007.
Values may be sent and summed in bfloat16 or wider, within the bound.
A program may use at most 384 MiB of HBM per device.

v0:
```python
import jax
import jax.numpy as jnp
from jax import lax
from jax.sharding import PartitionSpec as P


def on_device(tokens, right_blocks, left_blocks, chan_first, chan_second):
    rows_a = right_blocks.shape[0]
    block_len = right_blocks.shape[1]
    width = tokens.shape[1]
    count_k = chan_first.shape[0]
    count_m = chan_first.shape[1]
    x = tokens.reshape(rows_a, block_len, width)
    first = jnp.einsum("aob,abc->aoc", right_blocks, x, preferred_element_type=jnp.float32).astype(
        jnp.bfloat16
    )
    turned = jnp.einsum(
        "bxa,abc->xbc",
        left_blocks,
        lax.all_to_all(first, "seq", split_axis=1, concat_axis=0, tiled=True),
        preferred_element_type=jnp.float32,
    ).astype(jnp.bfloat16)
    back = lax.all_to_all(turned, "seq", split_axis=0, concat_axis=1, tiled=True)
    hidden = back.reshape(rows_a * block_len, width)
    gated = (tokens.astype(jnp.float32) * hidden.astype(jnp.float32)).astype(jnp.bfloat16)
    grouped = gated.reshape(rows_a * block_len, count_k, count_m)
    chan_mid = jnp.einsum(
        "kom,skm->sko", chan_first, grouped, preferred_element_type=jnp.float32
    ).astype(jnp.bfloat16)
    result = jnp.einsum("mok,skm->som", chan_second, chan_mid, preferred_element_type=jnp.float32)
    return result.reshape(rows_a * block_len, width).astype(jnp.bfloat16)


def solution(mesh):
    return jax.shard_map(
        on_device,
        mesh=mesh,
        in_specs=(P(("groups", "seq"), None), P("seq", None, None), P("seq", None, None), P(), P()),
        out_specs=P(("groups", "seq"), None),
        check_vma=False,
    )
```

profile of v0, /device:TPU:15, one launch (start us, length us, event | category | flops | bytes accessed | tf_op | source)
XLA Modules:
  0.0 1969.9 jit_solution(11058670894132006757)
XLA Ops:
  0.0 0.0 copy-start
  0.0 32.4 %convolution_convert_fusion.1 = bf16[16,512,2048]{2,1,0:T(8,128)(2,1)} fusion(bf16[16,512,512]{2,1,0:T(8,128)(2,1)} %param.6, bf16[16,512,2048]{2,1,0:T(8,128)(2,1)} %bitcast.29), kind=kOutput, calls=%fused_computation.10 | convolution fusion | flops 17196646400 | bytes 75497472 | tf_op jit(solution)/shard_map/aob,abc->aoc/dot_general | solution.py:14
  32.4 30.0 %copy.34 = bf16[16,512,2048]{2,0,1:T(8,128)(2,1)} copy(bf16[16,512,2048]{2,1,0:T(8,128)(2,1)} %convolution_convert_fusion.1) | data formatting | bytes 67108864 | tf_op jit(solution)/shard_map/convert_element_type | solution.py:14
  62.5 729.7 %all_to_all.27 = bf16[16,512,2048]{2,0,1:T(8,128)(2,1)} all-to-all(bf16[16,512,2048]{2,0,1:T(8,128)(2,1)} %copy.34), channel_id=1, replica_groups=mesh['groups'=2,'seq'=16] {'seq'}, dimensions={1} | all-to-all | bytes 67108864 | tf_op jit(solution)/shard_map/all_to_all | solution.py:20
  792.2 29.9 %copy.36 = bf16[16,16,32,2048]{3,2,1,0:T(8,128)(2,1)} copy(bf16[16,16,32,2048]{3,1,2,0:T(8,128)(2,1)} %bitcast.27) | data formatting | bytes 67108864 | tf_op jit(solution)/shard_map/all_to_all | solution.py:20
  822.1 54.8 %convert_bitcast_fusion.2 = bf16[256,32,2048]{0,2,1:T(8,128)(2,1)} fusion(bf16[32,256,256]{2,1,0:T(8,128)(2,1)} %param.7, bf16[256,32,2048]{2,1,0:T(8,128)(2,1)} %bitcast.26), kind=kOutput, calls=%fused_computation.8 | convolution fusion | flops 8606711808 | bytes 71303168 | tf_op jit(solution)/shard_map/bxa,abc->xbc/dot_general | solution.py:17
  876.9 47.1 %copy.38 = bf16[256,32,2048]{2,1,0:T(8,128)(2,1)} copy(bf16[256,32,2048]{0,2,1:T(8,128)(2,1)} %convert_bitcast_fusion.2) | data formatting | bytes 67108864 | tf_op jit(solution)/shard_map/convert_element_type | solution.py:22
  924.1 0.0 copy-start.1
  924.1 5.9 all-to-all-start.1
  930.0 0.0 copy-done.1
  930.0 0.8 copy.42
  930.8 721.3 %all-to-all-done.1 = bf16[256,32,2048]{2,1,0:T(8,128)(2,1)} async-done(((bf16[256,32,2048]{2,1,0:T(8,128)(2,1)}), bf16[256,32,2048]{2,1,0:T(8,128)(2,1)}, u32[]{:S(2)}, u32[]{:S(2)}) %all-to-all-start.1) | async-done | bytes 33554464 | tf_op jit(solution)/shard_map/all_to_all | solution.py:23
  1652.1 32.4 %convert_bitcast_fusion = f32[16,16,32,2048]{3,2,0,1:T(8,128)} fusion(bf16[16,16,32,2048]{3,2,1,0:T(8,128)(2,1)} %bitcast.12), kind=kLoop, calls=%fused_computation | loop fusion | flops 16777216 | bytes 100663296 | tf_op jit(solution)/shard_map/convert_element_type | solution.py:25
  1684.6 43.8 %copy.39 = f32[16,16,32,2048]{3,2,1,0:T(8,128)} copy(f32[16,16,32,2048]{3,2,0,1:T(8,128)} %convert_bitcast_fusion) | data formatting | bytes 134217728 | tf_op jit(solution)/shard_map/convert_element_type | solution.py:25
  1728.4 42.5 %fusion = bf16[8192,2048]{1,0:T(8,128)(2,1)} fusion(f32[16,16,32,2048]{3,2,1,0:T(8,128)} %copy.39, bf16[8192,2048]{1,0:T(8,128)(2,1)} %param.5), kind=kLoop, calls=%fused_computation.2 | loop fusion | flops 50331648 | bytes 134217728 | tf_op jit(solution)/shard_map/convert_element_type | solution.py:25
  1770.9 40.6 %copy.40 = bf16[8192,2048]{0,1:T(8,128)(2,1)} copy(bf16[8192,2048]{1,0:T(8,128)(2,1)} %fusion) | data formatting | bytes 67108864 | tf_op jit(solution)/shard_map/convert_element_type | solution.py:25
  1811.5 0.0 copy-done
  1811.5 23.3 %convolution_convert_fusion = bf16[32,8192,64]{1,2,0:T(8,128)(2,1)} fusion(bf16[32,64,64]{2,1,0:T(8,128)(2,1)S(1)} %copy-done, bf16[8192,32,64]{0,2,1:T(8,128)(2,1)} %bitcast.25), kind=kOutput, calls=%fused_computation.9 | convolution fusion | flops 2164260864 | bytes 67371008 | tf_op jit(solution)/shard_map/kom,skm->sko/dot_general | solution.py:27
  1834.8 61.5 %convert_bitcast_fusion.1 = bf16[8192,32,64]{0,1,2:T(8,128)(2,1)} fusion(bf16[64,32,32]{2,1,0:T(8,128)(2,1)S(1)} %copy.42, bf16[32,8192,64]{1,2,0:T(8,128)(2,1)} %convolution_convert_fusion), kind=kOutput, calls=%fused_computation.7 | convolution fusion | flops 1090519040 | bytes 67239936 | tf_op jit(solution)/shard_map/mok,skm->som/dot_general | solution.py:30
  1896.3 29.4 %copy.43 = bf16[8192,32,64]{0,2,1:T(8,128)(2,1)} copy(bf16[8192,32,64]{0,1,2:T(8,128)(2,1)} %convert_bitcast_fusion.1) | data formatting | bytes 67108864 | tf_op jit(solution)/shard_map/convert_element_type | solution.py:31
  1925.7 44.2 %copy.44 = bf16[8192,2048]{1,0:T(8,128)(2,1)} copy(bf16[8192,2048]{0,1:T(8,128)(2,1)} %bitcast.28) | data formatting | bytes 67108864 | tf_op jit(solution)/shard_map/convert_element_type | solution.py:31
Async XLA Ops:
  0.0 1811.5 %copy-start = (bf16[32,64,64]{2,1,0:T(8,128)(2,1)S(1)}, bf16[32,64,64]{2,1,0:T(8,128)(2,1)}, u32[]{:S(2)}) copy-start(bf16[32,64,64]{2,1,0:T(8,128)(2,1)} %param.8) | copy-start | bytes 786436
  924.1 6.0 copy-start.1
  924.1 728.1 %all-to-all-start.1 = ((bf16[256,32,2048]{2,1,0:T(8,128)(2,1)}), bf16[256,32,2048]{2,1,0:T(8,128)(2,1)}, u32[]{:S(2)}, u32[]{:S(2)}) async-start(bf16[256,32,2048]{2,1,0:T(8,128)(2,1)} %copy.38), calls=%async_computation.1 | async-start | bytes 67108864 | tf_op jit(solution)/shard_map/all_to_all | solution.py:23
where the time goes:
time: 1970 us
  blocking collectives  730 us (37%)
  waiting for transfers between devices  721 us (37%)
  local copies, waits for them, and re-layouts  266 us (14%)
  matrix products  172 us (9%)
  other arithmetic  75 us (4%)
    all_to_all x1, blocking collectives, on_device(): lax.all_to_all(first, 'seq', split_axis=1, concat_axis=0, tiled=True)  730 us
    all_to_all x1, waiting for transfers between devices, on_device(): lax.all_to_all(turned, 'seq', split_axis=0, concat_axis=1, tiled=True)  721 us
    convert_element_type x2, local copies, waits for them, and re-layouts, on_device(): return result.reshape(rows_a * block_len, width).astype(jnp.bfloat16)  73.6 us
    dot_general x1, matrix products, on_device(): jnp.einsum('mok,skm->som', chan_second, chan_mid, preferred_element_type=...  61.5 us
    dot_general x1, matrix products, on_device(): jnp.einsum('bxa,abc->xbc', left_blocks, lax.all_to_all(first, 'seq', spli...  54.8 us
    convert_element_type x1, local copies, waits for them, and re-layouts, on_device(): turned = jnp.einsum('bxa,abc->xbc', left_blocks, lax.all_to_all(first, 's...  47.1 us
    convert_element_type x1, local copies, waits for them, and re-layouts, on_device(): hidden.astype(jnp.float32)  43.8 us
    convert_element_type x1, other arithmetic, on_device(): (tokens.astype(jnp.float32) * hidden.astype(jnp.float32)).astype(jnp.bflo...  42.5 us
  transfers between devices with their start and end apart: 1, of which 1 were waited for; matrix products, arithmetic and copies ran while one was open for 0% of the time, Pallas kernels for 0%

commit v1 on v0

--- a/solution.py
+++ b/solution.py
@@ -20,7 +20,19 @@
         lax.all_to_all(first, "seq", split_axis=1, concat_axis=0, tiled=True),
         preferred_element_type=jnp.float32,
     ).astype(jnp.bfloat16)
-    back = lax.all_to_all(turned, "seq", split_axis=0, concat_axis=1, tiled=True)
+    ways, here = (lax.axis_size("seq"), lax.axis_index("seq"))
+    width_2 = turned.shape[0] // ways
+    dims = list(turned.shape)
+    dims[0] = width_2
+    height = dims[1]
+    dims[1] = height * ways
+    full = jnp.zeros(dims, turned.dtype)
+    for mask in range(ways):
+        part = lax.dynamic_slice_in_dim(turned, (here ^ mask) * width_2, width_2, axis=0)
+        if mask:
+            part = lax.ppermute(part, "seq", [(d, d ^ mask) for d in range(ways)])
+        full = lax.dynamic_update_slice_in_dim(full, part, (here ^ mask) * height, axis=1)
+    back = full
     hidden = back.reshape(rows_a * block_len, width)
     gated = (tokens.astype(jnp.float32) * hidden.astype(jnp.float32)).astype(jnp.bfloat16)
     grouped = gated.reshape(rows_a * block_len, count_k, count_m)

time: 1970 us -> 2350 us (1.19)
  the two profiles are of different devices: /device:TPU:15 before, /device:TPU:17 now
where the time goes in v1:
time: 2350 us; the launch traced here: 2340 us
  waiting for transfers between devices  1200 us (51%)
  local copies, waits for them, and re-layouts  717 us (31%)
  starting transfers between devices  206 us (9%)
  matrix products  142 us (6%)
  other arithmetic  75.1 us (3%)
    all_to_all x1, waiting for transfers between devices, on_device(): lax.all_to_all(first, 'seq', split_axis=1, concat_axis=0, tiled=True)  721 us
    ppermute x15, waiting for transfers between devices, on_device(): part = lax.ppermute(part, 'seq', [(d, d ^ mask) for d in range(ways)])  480 us
    dynamic_update_slice x17, local copies, waits for them, and re-layouts, on_device(): lax.dynamic_update_slice_in_dim(full, part, (here ^ mask) * height, axis=1)  425 us
    ppermute x15, starting transfers between devices, on_device(): part = lax.ppermute(part, 'seq', [(d, d ^ mask) for d in range(ways)])  199 us
    unnamed x35, local copies, waits for them, and re-layouts  116 us
    convert_element_type x2, local copies, waits for them, and re-layouts, on_device(): return result.reshape(rows_a * block_len, width).astype(jnp.bfloat16)  73.6 us
    dot_general x1, matrix products, on_device(): jnp.einsum('mok,skm->som', chan_second, chan_mid, preferred_element_type=...  61.8 us
  transfers between devices with their start and end apart: 16, of which 11 were waited for; matrix products, arithmetic and copies ran while one was open for 6% of the time, Pallas kernels for 0%

profile of v1, /device:TPU:17, one launch (start us, length us, event | category | flops | bytes accessed | tf_op | source)
XLA Modules:
  0.0 2342.1 jit_solution(17707304306989541762)
XLA Ops:
  0.0 32.4 %convolution_convert_fusion.1 = bf16[16,512,2048]{2,1,0:T(8,128)(2,1)} fusion(bf16[16,512,512]{2,1,0:T(8,128)(2,1)} %param.6, bf16[16,512,2048]{2,1,0:T(8,128)(2,1)} %bitcast.55), kind=kOutput, calls=%fused_computation.5 | convolution fusion | flops 17196646400 | bytes 75497472 | tf_op jit(solution)/shard_map/aob,abc->aoc/dot_general | solution.py:14
  32.4 30.0 %copy.18 = bf16[16,512,2048]{2,0,1:T(8,128)(2,1)} copy(bf16[16,512,2048]{2,1,0:T(8,128)(2,1)} %convolution_convert_fusion.1) | data formatting | bytes 67108864 | tf_op jit(solution)/shard_map/convert_element_type | solution.py:14
  62.5 7.1 all-to-all-start
  69.7 721.1 %all-to-all-done = bf16[16,512,2048]{2,0,1:T(8,128)(2,1)} async-done(((bf16[16,512,2048]{2,0,1:T(8,128)(2,1)}), bf16[16,512,2048]{2,0,1:T(8,128)(2,1)}, u32[]{:S(2)}, u32[]{:S(2)}) %all-to-all-start) | async-done | bytes 33554464 | tf_op jit(solution)/shard_map/all_to_all | solution.py:20
  790.8 22.9 copy.19
  813.7 24.5 %convolution_convert_fusion.2 = bf16[32,2048,256]{1,2,0:T(8,128)(2,1)} fusion(bf16[32,256,256]{2,1,0:T(8,128)(2,1)} %param.7, bf16[256,32,2048]{2,0,1:T(8,128)(2,1)} %bitcast.53), kind=kOutput, calls=%fused_computation.6 | convolution fusion | flops 8606711808 | bytes 71303168 | tf_op jit(solution)/shard_map/bxa,abc->xbc/dot_general | solution.py:17
  838.2 20.7 dynamic-slice_bitcast_fusion
  864.7 42.5 %collective-permute-done.1 = bf16[16,32,2048]{2,0,1:T(8,128)(2,1)S(1)} collective-permute-done((bf16[16,32,2048]{2,0,1:T(8,128)(2,1)}, bf16[16,32,2048]{2,0,1:T(8,128)(2,1)S(1)}, u32[]{:S(2)}, u32[]{:S(2)}) %collective-permute-start.1) | collective-permute-done | bytes 2097184 | tf_op jit(solution)/shard_map/ppermute | solution.py:33
  909.4 43.2 %collective-permute-done.2 = bf16[16,32,2048]{2,0,1:T(8,128)(2,1)S(1)} collective-permute-done((bf16[16,32,2048]{2,0,1:T(8,128)(2,1)S(1)}, bf16[16,32,2048]{2,0,1:T(8,128)(2,1)S(1)}, u32[]{:S(2)}, u32[]{:S(2)}) %collective-permute-start.2) | collective-permute-done | bytes 2097184 | tf_op jit(solution)/shard_map/ppermute | solution.py:33
  956.7 40.8 %copy.17 = bf16[8192,2048]{0,1:T(8,128)(2,1)} copy(bf16[8192,2048]{1,0:T(8,128)(2,1)} %param.5) | data formatting | bytes 67108864 | tf_op args[0]
  999.1 16.0 broadcast_in_dim.3
  1015.1 3.2 bitcast_dynamic-update-slice_fusion
  1019.8 3.2 constant_dynamic-update-slice_fusion.12
  1022.9 62.3 %collective-permute-done.5 = bf16[16,32,2048]{2,0,1:T(8,128)(2,1)} collective-permute-done((bf16[16,32,2048]{2,0,1:T(8,128)(2,1)}, bf16[16,32,2048]{2,0,1:T(8,128)(2,1)}, u32[]{:S(2)}, u32[]{:S(2)}) %collective-permute-start.5) | collective-permute-done | bytes 2097184 | tf_op jit(solution)/shard_map/ppermute | solution.py:33
  1085.3 4.6 collective-permute-start.10
  1091.3 38.9 %collective-permute-done.6 = bf16[16,32,2048]{2,0,1:T(8,128)(2,1)} collective-permute-done((bf16[16,32,2048]{2,0,1:T(8,128)(2,1)}, bf16[16,32,2048]{2,0,1:T(8,128)(2,1)}, u32[]{:S(2)}, u32[]{:S(2)}) %collective-permute-start.6) | collective-permute-done | bytes 2097184 | tf_op jit(solution)/shard_map/ppermute | solution.py:33
  1135.4 179.4 %collective-permute-start.13 = (bf16[16,32,2048]{2,0,1:T(8,128)(2,1)S(1)}, bf16[16,32,2048]{2,0,1:T(8,128)(2,1)S(1)}, u32[]{:S(2)}, u32[]{:S(2)}) collective-permute-start(bf16[16,32,2048]{2,0,1:T(8,128)(2,1)S(1)} %copy-done.2), channel_id=1, source_target_pairs={{0,14},{1,15},{2,12},{3,13},{4,10},{5,11},{6,8},{7,9},{8,6},{9,7},... | collective-permute-start | bytes 6291464 | tf_op jit(solution)/shard_map/ppermute | solution.py:33
  1318.0 84.8 %collective-permute-done.9 = bf16[16,32,2048]{2,0,1:T(8,128)(2,1)} collective-permute-done((bf16[16,32,2048]{2,0,1:T(8,128)(2,1)}, bf16[16,32,2048]{2,0,1:T(8,128)(2,1)}, u32[]{:S(2)}, u32[]{:S(2)}) %collective-permute-start.9) | collective-permute-done | bytes 2097184 | tf_op jit(solution)/shard_map/ppermute | solution.py:33
  1417.9 74.7 %collective-permute-done.10 = bf16[16,32,2048]{2,0,1:T(8,128)(2,1)S(1)} collective-permute-done((bf16[16,32,2048]{2,0,1:T(8,128)(2,1)S(1)}, bf16[16,32,2048]{2,0,1:T(8,128)(2,1)S(1)}, u32[]{:S(2)}, u32[]{:S(2)}) %collective-permute-start.10) | collective-permute-done | bytes 2097184 | tf_op jit(solution)/shard_map/ppermute | solution.py:33
  1494.0 44.7 %collective-permute-done.11 = bf16[16,32,2048]{2,0,1:T(8,128)(2,1)S(1)} collective-permute-done((bf16[16,32,2048]{2,0,1:T(8,128)(2,1)S(1)}, bf16[16,32,2048]{2,0,1:T(8,128)(2,1)S(1)}, u32[]{:S(2)}, u32[]{:S(2)}) %collective-permute-start.11) | collective-permute-done | bytes 2097184 | tf_op jit(solution)/shard_map/ppermute | solution.py:33
  1540.2 43.9 %collective-permute-done.12 = bf16[16,32,2048]{2,0,1:T(8,128)(2,1)S(1)} collective-permute-done((bf16[16,32,2048]{2,0,1:T(8,128)(2,1)S(1)}, bf16[16,32,2048]{2,0,1:T(8,128)(2,1)S(1)}, u32[]{:S(2)}, u32[]{:S(2)}) %collective-permute-start.12) | collective-permute-done | bytes 2097184 | tf_op jit(solution)/shard_map/ppermute | solution.py:33
  1585.6 44.5 %collective-permute-done.13 = bf16[16,32,2048]{2,0,1:T(8,128)(2,1)S(1)} collective-permute-done((bf16[16,32,2048]{2,0,1:T(8,128)(2,1)S(1)}, bf16[16,32,2048]{2,0,1:T(8,128)(2,1)S(1)}, u32[]{:S(2)}, u32[]{:S(2)}) %collective-permute-start.13) | collective-permute-done | bytes 2097184 | tf_op jit(solution)/shard_map/ppermute | solution.py:33
  1631.5 49.9 %copy.20 = bf16[16,512,2048]{1,0,2:T(8,128)(2,1)} copy(bf16[16,512,2048]{2,0,1:T(8,128)(2,1)} %constant_dynamic-update-slice_fusion) | data formatting | bytes 67108864 | tf_op jit(solution)/shard_map/dynamic_update_slice | solution.py:34
  1681.4 12.8 copy.21
  1694.2 341.4 %dynamic_update_slice.63 = bf16[16,512,2048]{1,0,2:T(8,128)(2,1)} dynamic-update-slice(bf16[16,512,2048]{1,0,2:T(8,128)(2,1)} %copy.20, bf16[16,32,2048]{1,0,2:T(8,128)(2,1)} %copy.21, s32[]{:T(128)} %constant.1.clone.1, s32[]{:T(128)S(6)} %select_n.127, s32[]{:T(128)} %constant.1.clone.1) | dynamic-update-slice | bytes 4194308 | tf_op jit(solution)/shard_map/dynamic_update_slice | solution.py:34
  2035.6 32.4 %convert_element_type.42 = f32[16,512,2048]{1,0,2:T(8,128)} convert(bf16[16,512,2048]{1,0,2:T(8,128)(2,1)} %dynamic_update_slice.63) | non-fusion elementwise | flops 16777216 | bytes 100663296 | tf_op jit(solution)/shard_map/convert_element_type | solution.py:37
  2068.0 72.6 %copy.26 = f32[256,8,16,512]{3,1,2,0:T(8,128)} copy(f32[256,8,16,512]{3,2,1,0:T(8,128)} %bitcast.25) | data formatting | bytes 134217728
  2140.6 42.7 %multiply_convert_fusion = bf16[8192,2048]{0,1:T(8,128)(2,1)} fusion(f32[8192,2048]{0,1:T(8,128)} %bitcast.27, bf16[8192,2048]{0,1:T(8,128)(2,1)} %copy.17), kind=kLoop, calls=%fused_computation | loop fusion | flops 50331648 | bytes 134217728 | tf_op jit(solution)/shard_map/convert_element_type | solution.py:37
  2183.3 23.0 convolution_convert_fusion
  2206.3 61.8 %convert_bitcast_fusion = bf16[8192,32,64]{0,1,2:T(8,128)(2,1)} fusion(bf16[64,32,32]{2,1,0:T(8,128)(2,1)S(1)} %copy-done.1, bf16[32,8192,64]{1,2,0:T(8,128)(2,1)} %convolution_convert_fusion), kind=kOutput, calls=%fused_computation.3 | convolution fusion | flops 1090519040 | bytes 67239936 | tf_op jit(solution)/shard_map/mok,skm->som/dot_general | solution.py:42
  2268.2 29.4 %copy.24 = bf16[8192,32,64]{0,2,1:T(8,128)(2,1)} copy(bf16[8192,32,64]{0,1,2:T(8,128)(2,1)} %convert_bitcast_fusion) | data formatting | bytes 67108864 | tf_op jit(solution)/shard_map/convert_element_type | solution.py:43
  2297.6 44.2 %copy.25 = bf16[8192,2048]{1,0:T(8,128)(2,1)} copy(bf16[8192,2048]{0,1:T(8,128)(2,1)} %bitcast.54) | data formatting | bytes 67108864 | tf_op jit(solution)/shard_map/convert_element_type | solution.py:43
  (65 shorter events, 45.9 us)
Async XLA Ops:
  0.0 2183.3 %copy-start = (bf16[32,64,64]{2,1,0:T(8,128)(2,1)S(1)}, bf16[32,64,64]{2,1,0:T(8,128)(2,1)}, u32[]{:S(2)}) copy-start(bf16[32,64,64]{2,1,0:T(8,128)(2,1)} %param.8) | copy-start | bytes 786436
  62.5 728.3 %all-to-all-start = ((bf16[16,512,2048]{2,0,1:T(8,128)(2,1)}), bf16[16,512,2048]{2,0,1:T(8,128)(2,1)}, u32[]{:S(2)}, u32[]{:S(2)}) async-start(bf16[16,512,2048]{2,0,1:T(8,128)(2,1)} %copy.18), calls=%async_computation | async-start | bytes 67108864 | tf_op jit(solution)/shard_map/all_to_all | solution.py:20
  858.9 4.9 collective-permute-start
  859.8 47.4 %collective-permute-start.1 = (bf16[16,32,2048]{2,0,1:T(8,128)(2,1)}, bf16[16,32,2048]{2,0,1:T(8,128)(2,1)S(1)}, u32[]{:S(2)}, u32[]{:S(2)}) collective-permute-start(bf16[16,32,2048]{2,0,1:T(8,128)(2,1)} %get-tuple-element.18), channel_id=1, source_target_pairs={{0,2},{1,3},{2,0},{3,1},{4,6},{5,7},{6,4},{7,5},{8,10},{9,11},{10,... | collective-permute-start | bytes 6291464 | tf_op jit(solution)/shard_map/ppermute | solution.py:33
  859.8 92.8 %collective-permute-start.2 = (bf16[16,32,2048]{2,0,1:T(8,128)(2,1)S(1)}, bf16[16,32,2048]{2,0,1:T(8,128)(2,1)S(1)}, u32[]{:S(2)}, u32[]{:S(2)}) collective-permute-start(bf16[16,32,2048]{2,0,1:T(8,128)(2,1)S(1)} %get-tuple-element.17), channel_id=1, source_target_pairs={{0,3},{1,2},{2,1},{3,0},{4,7},{5,6},{6,5},{7,4},{8,11},{9,10},{10,... | collective-permute-start | bytes 6291464 | tf_op jit(solution)/shard_map/ppermute | solution.py:33
  861.5 91.1 %collective-permute-start.3 = (bf16[16,32,2048]{2,0,1:T(8,128)(2,1)S(1)}, bf16[16,32,2048]{2,0,1:T(8,128)(2,1)S(1)}, u32[]{:S(2)}, u32[]{:S(2)}) collective-permute-start(bf16[16,32,2048]{2,0,1:T(8,128)(2,1)S(1)} %get-tuple-element.16), channel_id=1, source_target_pairs={{0,4},{1,5},{2,6},{3,7},{4,0},{5,1},{6,2},{7,3},{8,12},{9,13},{10,... | collective-permute-start | bytes 6291464 | tf_op jit(solution)/shard_map/ppermute | solution.py:33
  861.5 93.6 %collective-permute-start.4 = (bf16[16,32,2048]{2,0,1:T(8,128)(2,1)S(1)}, bf16[16,32,2048]{2,0,1:T(8,128)(2,1)S(1)}, u32[]{:S(2)}, u32[]{:S(2)}) collective-permute-start(bf16[16,32,2048]{2,0,1:T(8,128)(2,1)S(1)} %get-tuple-element.15), channel_id=1, source_target_pairs={{0,5},{1,4},{2,7},{3,6},{4,1},{5,0},{6,3},{7,2},{8,13},{9,12},{10,... | collective-permute-start | bytes 6291464 | tf_op jit(solution)/shard_map/ppermute | solution.py:33
  863.8 92.6 %copy-start.12 = (bf16[16,32,2048]{2,0,1:T(8,128)(2,1)}, bf16[16,32,2048]{2,0,1:T(8,128)(2,1)S(1)}, u32[]{:S(2)}) copy-start(bf16[16,32,2048]{2,0,1:T(8,128)(2,1)S(1)} %collective-permute-done) | copy-start | bytes 6291460
  863.8 221.4 %collective-permute-start.5 = (bf16[16,32,2048]{2,0,1:T(8,128)(2,1)}, bf16[16,32,2048]{2,0,1:T(8,128)(2,1)}, u32[]{:S(2)}, u32[]{:S(2)}) collective-permute-start(bf16[16,32,2048]{2,0,1:T(8,128)(2,1)} %get-tuple-element.14), channel_id=1, source_target_pairs={{0,6},{1,7},{2,4},{3,5},{4,2},{5,3},{6,0},{7,1},{8,14},{9,15},{10,... | collective-permute-start | bytes 6291464 | tf_op jit(solution)/shard_map/ppermute | solution.py:33
  907.2 49.2 %copy-start.14 = (bf16[16,32,2048]{2,0,1:T(8,128)(2,1)}, bf16[16,32,2048]{2,0,1:T(8,128)(2,1)S(1)}, u32[]{:S(2)}) copy-start(bf16[16,32,2048]{2,0,1:T(8,128)(2,1)S(1)} %collective-permute-done.1) | copy-start | bytes 6291460
  907.2 223.0 %collective-permute-start.6 = (bf16[16,32,2048]{2,0,1:T(8,128)(2,1)}, bf16[16,32,2048]{2,0,1:T(8,128)(2,1)}, u32[]{:S(2)}, u32[]{:S(2)}) collective-permute-start(bf16[16,32,2048]{2,0,1:T(8,128)(2,1)} %get-tuple-element.13), channel_id=1, source_target_pairs={{0,7},{1,6},{2,5},{3,4},{4,3},{5,2},{6,1},{7,0},{8,15},{9,14},{10,... | collective-permute-start | bytes 6291464 | tf_op jit(solution)/shard_map/ppermute | solution.py:33
  952.6 3.8 copy-start.10
  952.6 179.6 %collective-permute-start.7 = (bf16[16,32,2048]{2,0,1:T(8,128)(2,1)}, bf16[16,32,2048]{2,0,1:T(8,128)(2,1)}, u32[]{:S(2)}, u32[]{:S(2)}) collective-permute-start(bf16[16,32,2048]{2,0,1:T(8,128)(2,1)} %get-tuple-element.12), channel_id=1, source_target_pairs={{0,8},{1,9},{2,10},{3,11},{4,12},{5,13},{6,14},{7,15},{8,0},{9,1},... | collective-permute-start | bytes 6291464 | tf_op jit(solution)/shard_map/ppermute | solution.py:33
  952.6 3.8 copy-start.8
  952.6 182.8 %collective-permute-start.8 = (bf16[16,32,2048]{2,0,1:T(8,128)(2,1)}, bf16[16,32,2048]{2,0,1:T(8,128)(2,1)}, u32[]{:S(2)}, u32[]{:S(2)}) collective-permute-start(bf16[16,32,2048]{2,0,1:T(8,128)(2,1)} %get-tuple-element.11), channel_id=1, source_target_pairs={{0,9},{1,8},{2,11},{3,10},{4,13},{5,12},{6,15},{7,14},{8,1},{9,0},... | collective-permute-start | bytes 6291464 | tf_op jit(solution)/shard_map/ppermute | solution.py:33
  955.1 1.3 copy-start.6
  956.5 446.3 %collective-permute-start.9 = (bf16[16,32,2048]{2,0,1:T(8,128)(2,1)}, bf16[16,32,2048]{2,0,1:T(8,128)(2,1)}, u32[]{:S(2)}, u32[]{:S(2)}) collective-permute-start(bf16[16,32,2048]{2,0,1:T(8,128)(2,1)} %get-tuple-element.10), channel_id=1, source_target_pairs={{0,10},{1,11},{2,8},{3,9},{4,14},{5,15},{6,12},{7,13},{8,2},{9,3},... | collective-permute-start | bytes 6291464 | tf_op jit(solution)/shard_map/ppermute | solution.py:33
  956.7 40.8 %copy-start.15 = (bf16[64,32,32]{0,2,1:T(8,128)(2,1)S(1)}, bf16[64,32,32]{0,2,1:T(8,128)(2,1)}, u32[]{:S(2)}) copy-start(bf16[64,32,32]{0,2,1:T(8,128)(2,1)} %param.9) | copy-start | bytes 393220
  999.1 19.2 copy-start.13
  999.1 86.2 %copy-start.5 = (bf16[16,32,2048]{2,0,1:T(8,128)(2,1)S(1)}, bf16[16,32,2048]{2,0,1:T(8,128)(2,1)}, u32[]{:S(2)}) copy-start(bf16[16,32,2048]{2,0,1:T(8,128)(2,1)} %get-tuple-element.9) | copy-start | bytes 6291460
  999.1 90.8 %copy-start.11 = (bf16[16,32,2048]{2,0,1:T(8,128)(2,1)S(1)}, bf16[16,32,2048]{2,0,1:T(8,128)(2,1)}, u32[]{:S(2)}) copy-start(bf16[16,32,2048]{2,0,1:T(8,128)(2,1)} %copy-done.10) | copy-start | bytes 6291460
  999.1 131.1 %copy-start.4 = (bf16[16,32,2048]{2,0,1:T(8,128)(2,1)S(1)}, bf16[16,32,2048]{2,0,1:T(8,128)(2,1)}, u32[]{:S(2)}) copy-start(bf16[16,32,2048]{2,0,1:T(8,128)(2,1)} %get-tuple-element.8) | copy-start | bytes 6291460
  999.1 131.6 %copy-start.9 = (bf16[16,32,2048]{2,0,1:T(8,128)(2,1)S(1)}, bf16[16,32,2048]{2,0,1:T(8,128)(2,1)}, u32[]{:S(2)}) copy-start(bf16[16,32,2048]{2,0,1:T(8,128)(2,1)} %copy-done.8) | copy-start | bytes 6291460
  999.1 133.1 %copy-start.3 = (bf16[16,32,2048]{2,0,1:T(8,128)(2,1)S(1)}, bf16[16,32,2048]{2,0,1:T(8,128)(2,1)}, u32[]{:S(2)}) copy-start(bf16[16,32,2048]{2,0,1:T(8,128)(2,1)} %get-tuple-element.7) | copy-start | bytes 6291460
  999.1 134.9 %copy-start.7 = (bf16[16,32,2048]{2,0,1:T(8,128)(2,1)S(1)}, bf16[16,32,2048]{2,0,1:T(8,128)(2,1)}, u32[]{:S(2)}) copy-start(bf16[16,32,2048]{2,0,1:T(8,128)(2,1)} %copy-done.6) | copy-start | bytes 6291460
  999.1 136.3 %copy-start.2 = (bf16[16,32,2048]{2,0,1:T(8,128)(2,1)S(1)}, bf16[16,32,2048]{2,0,1:T(8,128)(2,1)}, u32[]{:S(2)}) copy-start(bf16[16,32,2048]{2,0,1:T(8,128)(2,1)} %get-tuple-element.6) | copy-start | bytes 6291460
  1085.3 407.3 %collective-permute-start.10 = (bf16[16,32,2048]{2,0,1:T(8,128)(2,1)S(1)}, bf16[16,32,2048]{2,0,1:T(8,128)(2,1)S(1)}, u32[]{:S(2)}, u32[]{:S(2)}) collective-permute-start(bf16[16,32,2048]{2,0,1:T(8,128)(2,1)S(1)} %copy-done.5), channel_id=1, source_target_pairs={{0,11},{1,10},{2,9},{3,8},{4,15},{5,14},{6,13},{7,12},{8,3},{9,2},... | collective-permute-start | bytes 6291464 | tf_op jit(solution)/shard_map/ppermute | solution.py:33
  1130.2 408.5 %collective-permute-start.11 = (bf16[16,32,2048]{2,0,1:T(8,128)(2,1)S(1)}, bf16[16,32,2048]{2,0,1:T(8,128)(2,1)S(1)}, u32[]{:S(2)}, u32[]{:S(2)}) collective-permute-start(bf16[16,32,2048]{2,0,1:T(8,128)(2,1)S(1)} %copy-done.4), channel_id=1, source_target_pairs={{0,12},{1,13},{2,14},{3,15},{4,8},{5,9},{6,10},{7,11},{8,4},{9,5},... | collective-permute-start | bytes 6291464 | tf_op jit(solution)/shard_map/ppermute | solution.py:33
  1132.2 451.9 %collective-permute-start.12 = (bf16[16,32,2048]{2,0,1:T(8,128)(2,1)S(1)}, bf16[16,32,2048]{2,0,1:T(8,128)(2,1)S(1)}, u32[]{:S(2)}, u32[]{:S(2)}) collective-permute-start(bf16[16,32,2048]{2,0,1:T(8,128)(2,1)S(1)} %copy-done.3), channel_id=1, source_target_pairs={{0,13},{1,12},{2,15},{3,14},{4,9},{5,8},{6,11},{7,10},{8,5},{9,4},... | collective-permute-start | bytes 6291464 | tf_op jit(solution)/shard_map/ppermute | solution.py:33
  1135.4 494.6 %collective-permute-start.13 = (bf16[16,32,2048]{2,0,1:T(8,128)(2,1)S(1)}, bf16[16,32,2048]{2,0,1:T(8,128)(2,1)S(1)}, u32[]{:S(2)}, u32[]{:S(2)}) collective-permute-start(bf16[16,32,2048]{2,0,1:T(8,128)(2,1)S(1)} %copy-done.2), channel_id=1, source_target_pairs={{0,14},{1,15},{2,12},{3,13},{4,10},{5,11},{6,8},{7,9},{8,6},{9,7},... | collective-permute-start | bytes 6291464 | tf_op jit(solution)/shard_map/ppermute | solution.py:33
  1402.8 278.6 %collective-permute-start.14 = (bf16[16,32,2048]{2,0,1:T(8,128)(2,1)S(1)}, bf16[16,32,2048]{2,0,1:T(8,128)(2,1)}, u32[]{:S(2)}, u32[]{:S(2)}) collective-permute-start(bf16[16,32,2048]{2,0,1:T(8,128)(2,1)S(1)} %get-tuple-element.5), channel_id=1, source_target_pairs={{0,15},{1,14},{2,13},{3,12},{4,11},{5,10},{6,9},{7,8},{8,7},{9,6},... | collective-permute-start | bytes 6291464 | tf_op jit(solution)/shard_map/ppermute | solution.py:33
  2183.3 23.0 copy-start.1
